TPU v7x, 256 devices: a whole 4x4x8 slice. The times are simulated.
256 devices in a mesh: frame: 32 (over z_hi, y, core), head: 8 (over z_lo, x).
Axes of the slice: x: 4, y: 4, z: 8 (z_hi: 4, z_lo: 2; z = z_hi * 2 + z_lo), core: 2. Of those that a mesh axis runs over, the one named last changes fastest.
Arguments:
- tokens: bfloat16 [8192, 3072], P('frame'), may hold values from -6 to 6
- w_qkv: bfloat16 [3, 3072, 3072], P(None, None, 'head'), may hold values from -0.109375 to 0.109375
- norm_gains: float32 [2, 3072], P(None, 'head'), may hold values from 0.8 to 2.5
- w_out: bfloat16 [3072, 3072], P('head'), may hold values from -0.15625 to 0.15625
- near_mask: int32 [64, 4], P('frame'), may hold values 0 or 1
- far_pattern: int32 [64, 64], P('frame'), may hold values from 0 to 1, as said below
- window: int32 [32], replicated, may hold values from 1 to 256, as said below
Outputs:
- layer_out: bfloat16 [8192, 3072], P('frame', 'head')
- checksum: float32 [8192], P('frame')
Inputs may be any that keep to these rules, and one draw needn't show every extreme that they name: `far_pattern`: 0 or 1; entries whose two blocks lie in slabs less than two apart are never read. Entry d is the window for slabs d apart; entry 0 is 256.
All inputs are finite; a program needn't handle non-finite values. No bound on the sum of `near_mask` on one device may be relied on, other than what follows from the above.
Results may differ from a plain program's by a relative error of at most 0.015.
Values may be sent and summed in bfloat16 or wider, within the bound.
A program may use at most 128 MiB of HBM per device.

v0:
```python
import jax
import jax.numpy as jnp
from jax import lax
from jax.sharding import PartitionSpec as P

D = 3072
HD = 128
BLK = 128


def with_halo(cells, sides, width):
    for axis, dim in sides:
        count = lax.axis_size(axis)
        ends = count - 1
        head = lax.slice_in_dim(cells, 0, width, axis=dim)
        tail = lax.slice_in_dim(cells, cells.shape[dim] - width, cells.shape[dim], axis=dim)
        cells = jnp.concatenate(
            [
                lax.ppermute(tail, axis, [(i, (i + 1) % count) for i in range(ends)]),
                cells,
                lax.ppermute(head, axis, [((i + 1) % count, i) for i in range(ends)]),
            ],
            axis=dim,
        )
    return cells


def normed_heads(values, gain_row):
    shaped = values.reshape(values.shape[0], -1, HD)
    factor = lax.rsqrt(jnp.mean(shaped * shaped, axis=-1, keepdims=True) + 1e-06)
    return shaped * factor * gain_row.reshape(-1, HD)


def lookup_columns(table_int, columns, table_width):
    onehot = (jnp.arange(table_width, dtype=jnp.int32)[:, None] == columns[None, :]).astype(
        jnp.float32
    )
    return jnp.dot(table_int.astype(jnp.float32), onehot)


def attend(totals, key_part, value_part, first_row, context, which_keys):
    queries, near_mask, far_pattern, window, frame_id, slab_rows, n_frame = context
    numer, denom = totals
    key_span = key_part.shape[0]
    n_blocks = near_mask.shape[0]
    key_index = first_row + jnp.arange(key_span, dtype=jnp.int32)
    key_slab = key_index // slab_rows
    key_pos = key_index % slab_rows
    distance = jnp.abs(key_slab - frame_id)
    far_sel = lookup_columns(far_pattern, key_index // BLK, far_pattern.shape[1])
    key_side = jnp.where(key_slab < frame_id, 0, 1)
    near_sel = lookup_columns(near_mask, key_side * n_blocks + key_pos // BLK, 2 * n_blocks)
    if which_keys == "near":
        chosen = jnp.where(distance == 0, 1.0, jnp.where(distance == 1, near_sel, 0.0))
    else:
        chosen = jnp.where(distance >= 2, far_sel, 0.0)
    chosen = jnp.broadcast_to(chosen[:, None, :], (n_blocks, BLK, key_span)).reshape(
        slab_rows, key_span
    )
    inside = (key_index >= 0) & (key_index < slab_rows * n_frame)
    slab_steps = jnp.arange(n_frame, dtype=jnp.int32)
    key_limit = jnp.sum(
        jnp.where(slab_steps[:, None] == distance[None, :], window[:, None], 0), axis=0
    )
    position = jnp.arange(slab_rows, dtype=jnp.int32)
    allowed = (
        (chosen > 0.5)
        & inside[None, :]
        & (jnp.abs(position[:, None] - key_pos[None, :]) < key_limit[None, :])
    )
    key_heads = key_part.reshape(key_span, -1, HD)
    value_heads = value_part.reshape(key_span, -1, HD)
    scores = jnp.einsum("qhd,khd->hqk", queries, key_heads, preferred_element_type=jnp.float32)
    weights = jnp.where(allowed[None], jnp.exp(scores), 0.0)
    numer = numer + jnp.einsum(
        "hqk,khd->qhd",
        weights.astype(jnp.bfloat16),
        value_heads,
        preferred_element_type=jnp.float32,
    )
    denom = denom + jnp.sum(weights, axis=-1)
    return (numer, denom)


def per_device(tokens, w_qkv, norm_gains, w_out, near_mask, far_pattern, window):
    slab_rows = tokens.shape[0]
    frame_id = lax.axis_index("frame")
    n_frame = lax.axis_size("frame")
    query = jnp.dot(tokens, w_qkv[0], preferred_element_type=jnp.float32)
    key_full = jnp.dot(tokens, w_qkv[1], preferred_element_type=jnp.float32)
    value_full = jnp.dot(tokens, w_qkv[2], preferred_element_type=jnp.float32)
    queries = (normed_heads(query, norm_gains[0]) * HD ** (-0.5)).astype(jnp.bfloat16)
    keys_flat = normed_heads(key_full, norm_gains[1]).astype(jnp.bfloat16).reshape(slab_rows, -1)
    values_flat = value_full.astype(jnp.bfloat16)
    head_count = queries.shape[1]
    context = (queries, near_mask, far_pattern, window, frame_id, slab_rows, n_frame)
    start_totals = (
        jnp.zeros((slab_rows, head_count, HD), jnp.float32),
        jnp.zeros((head_count, slab_rows), jnp.float32),
    )
    stacked = jnp.stack([keys_flat, values_flat])
    widened = with_halo(stacked, (("frame", 1),), slab_rows)
    totals = attend(
        start_totals, widened[0], widened[1], (frame_id - 1) * slab_rows, context, "near"
    )
    totals = attend(
        totals,
        lax.all_gather(keys_flat, "frame", axis=0, tiled=True),
        lax.all_gather(values_flat, "frame", axis=0, tiled=True),
        jnp.int32(0),
        context,
        "far",
    )
    numer, denom = totals
    attended = (numer / denom.T[:, :, None]).reshape(slab_rows, -1).astype(jnp.bfloat16)
    full_cols = lax.psum_scatter(
        lax.dot_general(
            w_out, attended, (((0,), (1,)), ((), ())), preferred_element_type=jnp.float32
        ).astype(jnp.bfloat16),
        "head",
        scatter_dimension=0,
        tiled=True,
    ).astype(jnp.float32)
    full_rows = full_cols.T
    layer_out = full_rows.astype(jnp.bfloat16)
    checksum = lax.psum(jnp.sum(full_rows, axis=1) * D ** (-0.5), "head")
    return (layer_out, checksum)


def solution(mesh):
    in_specs = (
        P("frame", None),
        P(None, None, "head"),
        P(None, "head"),
        P("head", None),
        P("frame", None),
        P("frame", None),
        P(),
    )
    out_specs = (P("frame", "head"), P("frame"))
    return jax.shard_map(
        per_device, mesh=mesh, in_specs=in_specs, out_specs=out_specs, check_vma=False
    )
```

profile of v0, /device:TPU:8, one launch (start us, length us, event | category | flops | bytes accessed | tf_op | source)
XLA Modules:
  0.0 266.5 jit_solution(1134250349421031782)
XLA Ops:
  7.2 0.0 copy-start
  7.2 0.0 all-gather.5.cloned.1.call-start
  7.2 5.1 %slice_bitcast_fusion = (bf16[384,3072]{0,1:T(8,128)(2,1)}, bf16[384,3072]{0,1:T(8,128)(2,1)}) fusion(bf16[3,3072,384]{2,1,0:T(8,128)(2,1)} %param.8), kind=kLoop, calls=%fused_computation.17 | loop fusion | bytes 9437184 | tf_op jit(solution)/shard_map/dot_general | solution.py:89
  12.4 4.3 %copy.37 = bf16[384,3072]{1,0:T(8,128)(2,1)} copy(bf16[384,3072]{0,1:T(8,128)(2,1)} %get-tuple-element.5) | data formatting | bytes 4718592 | tf_op jit(solution)/shard_map/dot_general | solution.py:90
  16.7 3.0 %multiply_reduce_fusion.1 = (f32[256,3]{0,1:T(4,128)S(1)}, f32[256,3,128]{0,2,1:T(8,128)S(1)}) fusion(bf16[3,128,3072]{2,1,0:T(8,128)(2,1)} %bitcast.69, bf16[256,3072]{1,0:T(8,128)(2,1)} %param.7), kind=kOutput, calls=%fused_computation.50 | convolution fusion | flops 604175616 | bytes 4328448 | tf_op jit(solution)/shard_map/dot_general | solution.py:90
  19.6 0.8 multiply_convert_fusion.1
  20.4 0.0 all-gather.5.cloned.1.call-update
  20.5 0.0 copy-start.3
  20.5 0.0 all-gather.3.cloned.1.call-start
  20.5 3.8 %fusion.27 = bf16[256,384]{1,0:T(8,128)(2,1)} fusion(bf16[256,3072]{1,0:T(8,128)(2,1)} %param.7, bf16[3,3072,384]{2,1,0:T(8,128)(2,1)} %param.8), kind=kOutput, calls=%fused_computation.34 | convolution fusion | flops 604078080 | bytes 4128768 | tf_op jit(solution)/shard_map/dot_general | solution.py:91
  24.4 0.0 all-gather.3.cloned.1.call-update
  24.4 0.0 reduce-scatter.4.cloned.1.call-start
  24.4 0.2 copy.38
  24.6 1.7 pad_maximum_fusion.1
  26.3 1.9 collective-permute-start.1
  28.3 2.6 collective-permute-start
  30.9 0.0 copy-start.9
  30.9 0.0 copy-start.10
  30.9 4.3 %copy.40 = bf16[384,3072]{1,0:T(8,128)(2,1)} copy(bf16[384,3072]{0,1:T(8,128)(2,1)} %get-tuple-element.4) | data formatting | bytes 4718592 | tf_op jit(solution)/shard_map/dot_general | solution.py:89
  35.3 0.2 select_reduce_fusion
  35.5 0.4 fusion.7
  36.0 3.8 %fusion.8 = pred[256,8192]{1,0:T(8,128)(4,1)} fusion(s32[8192]{0:T(1024)S(1)} %select_reduce_fusion, s32[8192]{0:T(1024)S(1)} %fusion.35, pred[8192]{0:T(1024)(128)(4,1)S(1)} %iota_compare_fusion.4, pred[2,8192]{1,0:T(4,128)(4,1)S(1)} %fusion.7), kind=kLoop, calls=%fused_computation.10 | loop fusion | flops 10485760 | bytes 2187264 | tf_op jit(solution)/shard_map/and | solution.py:67
  39.8 0.1 select_reduce_fusion.1
  39.9 0.1 fusion.32
  40.1 0.9 fusion.34
  41.0 3.0 %multiply_reduce_fusion = (f32[256,3]{0,1:T(4,128)S(1)}, f32[256,3,128]{0,2,1:T(8,128)}) fusion(bf16[3,128,3072]{2,1,0:T(8,128)(2,1)S(1)} %bitcast.68, bf16[256,3072]{1,0:T(8,128)(2,1)} %param.7), kind=kOutput, calls=%fused_computation.48 | convolution fusion | flops 604175616 | bytes 4328448 | tf_op jit(solution)/shard_map/dot_general | solution.py:89
  44.0 0.0 collective-permute-done.1
  44.1 0.0 collective-permute-done
  44.1 0.1 pad_maximum_fusion
  44.2 0.1 fusion.66
  44.3 1.1 copy.39
  45.4 0.3 copy.41
  45.7 0.0 copy-start.7
  45.7 3.2 %fusion.13 = (f32[3,256]{1,0:T(4,128)S(1)}, f32[3,256,768]{2,1,0:T(8,128)}) fusion(pred[256,768]{1,0:T(8,128)(4,1)} %fusion.34, bf16[768,3,128]{0,2,1:T(8,128)(2,1)S(1)} %bitcast.70, f32[256,3,128]{0,2,1:T(8,128)} %get-tuple-element.11, f32[3,128]{1,0:T(4,128)S(1)} %bitcast.78, f32[256,3]{0,1:T(4,128)S(1)} %add_rsqrt_fusion), kind=kOutput, calls=%fused_computation.21 | convolution fusion | flops 152567040 | bytes 3546624 | tf_op jit(solution)/shard_map/qhd,khd->hqk/dot_general | solution.py:73
  48.9 50.5 %all-gather.5.cloned.1.call-done = bf16[8192,384]{0,1:T(8,128)(2,1)} async-done(((bf16[256,384]{0,1:T(8,128)(2,1)}), bf16[8192,384]{0,1:T(8,128)(2,1)}) %all-gather.5.cloned.1.call-update) | async-done | bytes 6291472 | tf_op jit(solution)/shard_map/all_gather | solution.py:108
  99.4 14.9 %fusion = (f32[3,256]{1,0:T(4,128)S(1)}, f32[3,256,8192]{2,1,0:T(8,128)}) fusion(pred[256,8192]{1,0:T(8,128)(4,1)} %fusion.8, bf16[8192,3,128]{0,2,1:T(8,128)(2,1)} %bitcast.81, f32[256,3,128]{0,2,1:T(8,128)S(1)} %copy-done.7, f32[3,128]{1,0:T(4,128)S(1)} %bitcast.79, f32[256,3]{0,1:T(4,128)S(1)} %add_rsqrt_fusion), kind=kOutput, calls=%fused_computation.1 | convolution fusion | flops 1623588096 | bytes 33955328 | tf_op jit(solution)/shard_map/qhd,khd->hqk/dot_general | solution.py:73
  114.3 56.0 %all-gather.3.cloned.1.call-done = bf16[8192,384]{1,0:T(8,128)(2,1)} async-done(((bf16[256,384]{1,0:T(8,128)(2,1)}), bf16[8192,384]{1,0:T(8,128)(2,1)}) %all-gather.3.cloned.1.call-update) | async-done | bytes 6291472 | tf_op jit(solution)/shard_map/all_gather | solution.py:109
  170.3 8.5 %copy.44 = bf16[8192,384]{0,1:T(8,128)(2,1)} copy(bf16[8192,384]{1,0:T(8,128)(2,1)} %all-gather.3.cloned.1.call-done) | data formatting | bytes 12582912 | tf_op jit(solution)/shard_map/all_gather | solution.py:109
  178.8 13.7 %fusion.2 = f32[3,128,256]{2,1,0:T(8,128)} fusion(bf16[8192,3,128]{0,2,1:T(8,128)(2,1)} %bitcast.67, f32[3,256,8192]{2,1,0:T(8,128)} %get-tuple-element.15, pred[256,8192]{1,0:T(8,128)(4,1)} %fusion.8), kind=kOutput, calls=%fused_computation.3 | convolution fusion | flops 1623195648 | bytes 33947648 | tf_op jit(solution)/shard_map/hqk,khd->qhd/dot_general | solution.py:75
  192.5 2.3 fusion.24
  194.8 2.2 fusion.9
  196.9 2.6 copy.51
  199.5 0.0 reduce-scatter.4.cloned.1.call-update
  199.6 41.9 %reduce-scatter.4.cloned.1.call-done = bf16[384,256]{1,0:T(8,128)(2,1)} async-done(((bf16[3072,256]{1,0:T(8,128)(2,1)}), bf16[384,256]{1,0:T(8,128)(2,1)}) %reduce-scatter.4.cloned.1.call-update) | async-done | bytes 196624
  241.4 1.1 copy.52
  242.5 0.0 copy-start.5
  242.5 0.1 convert_reduce_fusion
  242.7 17.3 %psum.7 = f32[256]{0:T(256)} all-reduce(f32[256]{0:T(256)S(1)} %broadcast_multiply_fusion), channel_id=1, replica_groups=mesh['frame'=32,'head'=8] {'head'}, use_global_device_ids=true, to_apply=%region_8.9 | all-reduce | flops 256 | bytes 2048 | tf_op jit(solution)/shard_map/psum | solution.py:126
  (32 shorter events, 0.2 us)
Async XLA Ops:
  7.2 187.6 %copy-start = (bf16[384,3072]{1,0:T(8,128)(2,1)S(1)}, bf16[384,3072]{1,0:T(8,128)(2,1)}, u32[]{:S(2)}) copy-start(bf16[384,3072]{1,0:T(8,128)(2,1)} %param.10) | copy-start | bytes 7077892
  7.2 92.2 %all-gather.5.cloned.1.call-start = ((), (), s32[]{:S(2)}) async-start(), calls=%async_computation.2 | async-start | bytes 6488064 | tf_op jit(solution)/shard_map/all_gather | solution.py:108
  12.3 4.3 %copy-start.8 = (f32[2,384]{1,0:T(2,128)S(1)}, f32[2,384]{1,0:T(2,128)}, u32[]{:S(2)}) copy-start(f32[2,384]{1,0:T(2,128)} %param.9) | copy-start | bytes 9220
  20.5 4.0 %copy-start.3 = (bf16[256,3,128]{0,2,1:T(8,128)(2,1)S(1)}, bf16[256,3,128]{0,2,1:T(8,128)(2,1)}, u32[]{:S(2)}) copy-start(bf16[256,3,128]{0,2,1:T(8,128)(2,1)} %multiply_convert_fusion.1) | copy-start | bytes 589828
  20.5 149.8 %all-gather.3.cloned.1.call-start = ((), (), s32[]{:S(2)}) async-start(), calls=%async_computation.1 | async-start | bytes 6488064 | tf_op jit(solution)/shard_map/all_gather | solution.py:109
  24.4 217.1 %reduce-scatter.4.cloned.1.call-start = ((), (), s32[]{:S(2)}) async-start(), calls=%async_computation.3 | async-start | bytes 1769472
  26.3 17.7 %collective-permute-start.1 = (bf16[2,256,384]{2,1,0:T(8,128)(2,1)}, bf16[2,256,384]{2,1,0:T(8,128)(2,1)S(1)}, u32[]{:S(2)}, u32[]{:S(2)}) collective-permute-start(bf16[2,256,384]{2,1,0:T(8,128)(2,1)} %pad_maximum_fusion.1), channel_id=1, source_target_pairs={{8,0},{16,8},{24,16},{32,24},{40,32},{48,40},{56,48},{64,56},{72,6... | collective-permute-start | bytes 1179656 | tf_op jit(solution)/shard_map/ppermute | solution.py:21
  28.3 15.8 %collective-permute-start = (bf16[2,256,384]{2,1,0:T(8,128)(2,1)}, bf16[2,256,384]{2,1,0:T(8,128)(2,1)S(1)}, u32[]{:S(2)}, u32[]{:S(2)}) collective-permute-start(bf16[2,256,384]{2,1,0:T(8,128)(2,1)} %pad_maximum_fusion.1), channel_id=1, source_target_pairs={{0,8},{8,16},{16,24},{24,32},{32,40},{40,48},{48,56},{56,64},{64,7... | collective-permute-start | bytes 1179656 | tf_op jit(solution)/shard_map/ppermute | solution.py:19
  30.9 4.4 %copy-start.9 = (s32[32]{0:T(128)S(1)}, s32[32]{0:T(128)}, u32[]{:S(2)}) copy-start(s32[32]{0:T(128)} %param.13) | copy-start | bytes 388
  30.9 4.6 %copy-start.10 = (s32[2,64]{1,0:T(2,128)S(1)}, s32[2,64]{1,0:T(2,128)}, u32[]{:S(2)}) copy-start(s32[2,64]{1,0:T(2,128)} %param.12) | copy-start | bytes 1540
  35.2 4.8 %copy-start.11 = (s32[2,4]{1,0:T(2,128)S(1)}, s32[2,4]{1,0:T(2,128)}, u32[]{:S(2)}) copy-start(s32[2,4]{1,0:T(2,128)} %param.11) | copy-start | bytes 100
  35.2 5.8 %copy-start.1 = (bf16[384,3072]{1,0:T(8,128)(2,1)S(1)}, bf16[384,3072]{1,0:T(8,128)(2,1)}, u32[]{:S(2)}) copy-start(bf16[384,3072]{1,0:T(8,128)(2,1)} %copy.40) | copy-start | bytes 7077892
  41.0 3.1 %copy-start.2 = (bf16[256,384]{1,0:T(8,128)(2,1)S(1)}, bf16[256,384]{1,0:T(8,128)(2,1)}, u32[]{:S(2)}) copy-start(bf16[256,384]{1,0:T(8,128)(2,1)} %fusion.27) | copy-start | bytes 589828
  45.7 53.7 %copy-start.7 = (f32[256,3,128]{0,2,1:T(8,128)S(1)}, f32[256,3,128]{0,2,1:T(8,128)}, u32[]{:S(2)}) copy-start(f32[256,3,128]{0,2,1:T(8,128)} %get-tuple-element.11) | copy-start | bytes 1179652
  178.8 13.7 %copy-start.4 = (pred[256,768]{1,0:T(8,128)(4,1)S(1)}, pred[256,768]{1,0:T(8,128)(4,1)}, u32[]{:S(2)}) copy-start(pred[256,768]{1,0:T(8,128)(4,1)} %fusion.34) | copy-start | bytes 589828
  178.8 13.7 %copy-start.6 = (bf16[1,768,384]{1,2,0:T(8,128)(2,1)S(1)}, bf16[1,768,384]{1,2,0:T(8,128)(2,1)}, u32[]{:S(2)}) copy-start(bf16[1,768,384]{1,2,0:T(8,128)(2,1)} %copy.39) | copy-start | bytes 1769476
  242.5 17.4 %copy-start.5 = (bf16[384,256]{0,1:T(8,128)(2,1)}, bf16[384,256]{0,1:T(8,128)(2,1)S(1)}, u32[]{:S(2)}) copy-start(bf16[384,256]{0,1:T(8,128)(2,1)S(1)} %copy.52) | copy-start | bytes 589828
Sparse Core Ops, SparseCore 0:
  20.6 78.7 all-gather.4
  102.5 67.7 all-gather.2
  199.7 41.7 reduce-scatter.3
where the time goes:
time: 267 us; the launch traced here: 266 us
  waiting for transfers between devices  148 us (55%)
  matrix products  46.6 us (17%)
  local copies, waits for them, and re-layouts  27.6 us (10%)
  blocking collectives  17.3 us (6%)
  between operations  14 us (5%)
  other arithmetic  7.97 us (3%)
  starting transfers between devices  4.62 us (2%)
    all_gather x1, waiting for transfers between devices, per_device(): lax.all_gather(values_flat, 'frame', axis=0, tiled=True)  56 us
    all_gather x1, waiting for transfers between devices, per_device(): lax.all_gather(keys_flat, 'frame', axis=0, tiled=True)  50.5 us
    unnamed x4, waiting for transfers between devices  41.9 us
    dot_general x2, matrix products, attend(): jnp.einsum('qhd,khd->hqk', queries, key_heads, preferred_element_type=jnp...  18.1 us
    psum x1, blocking collectives, per_device(): checksum = lax.psum(jnp.sum(full_rows, axis=1) * D ** (-0.5), 'head')  17.3 us
    dot_general x2, matrix products, attend(): jnp.einsum('hqk,khd->qhd', weights.astype(jnp.bfloat16), value_heads, pre...  15.9 us
    dot_general x2, local copies, waits for them, and re-layouts, per_device(): query = jnp.dot(tokens, w_qkv[0], preferred_element_type=jnp.float32)  9.4 us
    all_gather x1, local copies, waits for them, and re-layouts, per_device(): lax.all_gather(values_flat, 'frame', axis=0, tiled=True)  8.53 us
  transfers between devices with their start and end apart: 5, of which 3 were waited for; matrix products, arithmetic and copies ran while one was open for 14% of the time, Pallas kernels for 0%

commit v1 on v0

--- a/solution.py
+++ b/solution.py
@@ -106,7 +106,9 @@
     totals = attend(
         totals,
         lax.all_gather(keys_flat, "frame", axis=0, tiled=True),
-        lax.all_gather(values_flat, "frame", axis=0, tiled=True),
+        jnp.concatenate(
+            lax.all_to_all(jnp.stack([values_flat] * lax.axis_size("frame")), "frame", 0, 0), axis=0
+        ),
         jnp.int32(0),
         context,
         "far",

time: 267 us -> 332 us (1.24)
  waiting for transfers between devices: 148 us -> 188 us
  local copies, waits for them, and re-layouts: 27.6 us -> 42.9 us
  starting transfers between devices: 4.62 us -> 16.3 us
    all_to_all x0 -> x1, waiting for transfers between devices: none -> 125 us  [per_device(): lax.all_to_all(jnp.stack([values_flat] * lax.axis_size('frame')), 'frame'...]
    all_gather x1 -> x0, waiting for transfers between devices: 56 us -> none  [per_device(): lax.all_gather(values_flat, 'frame', axis=0, tiled=True)]
    all_gather x1, waiting for transfers between devices: 50.5 us -> 0.01 us  [per_device(): lax.all_gather(keys_flat, 'frame', axis=0, tiled=True)]
    another operation x0 -> x2, local copies, waits for them, and re-layouts: none -> 13.9 us  [the longest x1 10.5 us: attend(): value_heads = value_part.reshape(key_span, -1, HD)]
    all_to_all x0 -> x1, starting transfers between devices: none -> 11.7 us  [per_device(): lax.all_to_all(jnp.stack([values_flat] * lax.axis_size('frame')), 'frame'...]
    unnamed x4 -> x3, waiting for transfers between devices: 41.9 us -> 52.8 us
    ppermute x1, waiting for transfers between devices: 0.01 us -> 10.2 us  [with_halo(): lax.ppermute(head, axis, [((i + 1) % count, i) for i in range(ends)])]
    all_to_all x0 -> x1, local copies, waits for them, and re-layouts: none -> 9 us  [per_device(): lax.all_to_all(jnp.stack([values_flat] * lax.axis_size('frame')), 'frame'...]
  transfers between devices with their start and end apart: 5 -> 5, of which waited for: 3 -> 3; matrix products, arithmetic and copies ran while one was open for 14% -> 16% of each run, Pallas kernels for 0% -> 0%
where the time goes in v1:
time: 332 us; the launch traced here: 331 us
  waiting for transfers between devices  188 us (57%)
  matrix products  45.3 us (14%)
  local copies, waits for them, and re-layouts  42.9 us (13%)
  blocking collectives  17.4 us (5%)
  starting transfers between devices  16.3 us (5%)
  between operations  14.3 us (4%)
  other arithmetic  7.05 us (2%)
    all_to_all x1, waiting for transfers between devices, per_device(): lax.all_to_all(jnp.stack([values_flat] * lax.axis_size('frame')), 'frame'...  125 us
    unnamed x3, waiting for transfers between devices  52.8 us
    dot_general x2, matrix products, attend(): jnp.einsum('qhd,khd->hqk', queries, key_heads, preferred_element_type=jnp...  18.1 us
    psum x1, blocking collectives, per_device(): checksum = lax.psum(jnp.sum(full_rows, axis=1) * D ** (-0.5), 'head')  17.4 us
    dot_general x2, matrix products, attend(): jnp.einsum('hqk,khd->qhd', weights.astype(jnp.bfloat16), value_heads, pre...  15.1 us
    all_to_all x1, starting transfers between devices, per_device(): lax.all_to_all(jnp.stack([values_flat] * lax.axis_size('frame')), 'frame'...  11.7 us
    another operation x1, local copies, waits for them, and re-layouts, attend(): value_heads = value_part.reshape(key_span, -1, HD)  10.5 us
    ppermute x1, waiting for transfers between devices, with_halo(): lax.ppermute(head, axis, [((i + 1) % count, i) for i in range(ends)])  10.2 us
  transfers between devices with their start and end apart: 5, of which 3 were waited for; matrix products, arithmetic and copies ran while one was open for 16% of the time, Pallas kernels for 0%

profile of v1, /device:TPU:8, one launch (start us, length us, event | category | flops | bytes accessed | tf_op | source)
XLA Modules:
  0.0 331.0 jit_solution(10883477998026256964)
XLA Ops:
  7.2 0.0 copy-start
  7.2 3.3 fusion.27
  10.5 0.1 copy.45
  10.6 3.4 %stack.8 = bf16[32,256,384]{1,2,0:T(8,128)(2,1)} broadcast(bf16[256,384]{0,1:T(8,128)(2,1)S(1)} %copy.45), dimensions={1,2} | broadcast | bytes 6488064 | tf_op jit(solution)/shard_map/stack | solution.py:110
  14.0 11.7 %all-to-all-start = ((bf16[32,256,384]{1,2,0:T(8,128)(2,1)}), bf16[32,256,384]{1,2,0:T(8,128)(2,1)}, u32[]{:S(2)}, u32[]{:S(2)}) async-start(bf16[32,256,384]{1,2,0:T(8,128)(2,1)} %stack.8), calls=%async_computation | async-start | bytes 12582912 | tf_op jit(solution)/shard_map/all_to_all | solution.py:110
  25.7 0.0 all-gather.2.cloned.1.call-start
  25.8 5.0 %slice_bitcast_fusion = (bf16[384,3072]{0,1:T(8,128)(2,1)}, bf16[384,3072]{0,1:T(8,128)(2,1)}) fusion(bf16[3,3072,384]{2,1,0:T(8,128)(2,1)} %param.8), kind=kLoop, calls=%fused_computation.17 | loop fusion | bytes 9437184 | tf_op jit(solution)/shard_map/dot_general | solution.py:89
  30.7 4.3 %copy.38 = bf16[384,3072]{1,0:T(8,128)(2,1)} copy(bf16[384,3072]{0,1:T(8,128)(2,1)} %get-tuple-element.5) | data formatting | bytes 4718592 | tf_op jit(solution)/shard_map/dot_general | solution.py:90
  35.0 3.0 multiply_reduce_fusion.1
  38.0 0.0 copy-done.6
  38.1 0.8 multiply_convert_fusion.1
  38.9 0.0 all-gather.2.cloned.1.call-update
  38.9 0.0 reduce-scatter.4.cloned.1.call-start
  38.9 1.1 copy.39
  40.0 0.8 pad_maximum_fusion.1
  40.8 2.0 collective-permute-start.1
  42.9 2.5 collective-permute-start
  45.4 0.0 copy-start.7
  45.4 0.0 copy-start.8
  45.4 4.3 %copy.41 = bf16[384,3072]{1,0:T(8,128)(2,1)} copy(bf16[384,3072]{0,1:T(8,128)(2,1)} %get-tuple-element.4) | data formatting | bytes 4718592 | tf_op jit(solution)/shard_map/dot_general | solution.py:89
  49.8 0.2 select_reduce_fusion
  50.0 0.4 fusion.7
  50.5 3.8 %fusion.8 = pred[256,8192]{1,0:T(8,128)(4,1)} fusion(s32[8192]{0:T(1024)S(1)} %select_reduce_fusion, s32[8192]{0:T(1024)S(1)} %fusion.35, pred[8192]{0:T(1024)(128)(4,1)S(1)} %iota_compare_fusion.4, pred[2,8192]{1,0:T(4,128)(4,1)S(1)} %fusion.7), kind=kLoop, calls=%fused_computation.10 | loop fusion | flops 10485760 | bytes 2187264 | tf_op jit(solution)/shard_map/and | solution.py:67
  54.4 0.1 select_reduce_fusion.1
  54.5 0.1 fusion.32
  54.6 0.9 fusion.34
  55.5 3.0 multiply_reduce_fusion
  58.6 10.2 %collective-permute-done.1 = bf16[2,256,384]{2,1,0:T(8,128)(2,1)S(1)} collective-permute-done((bf16[2,256,384]{2,1,0:T(8,128)(2,1)}, bf16[2,256,384]{2,1,0:T(8,128)(2,1)S(1)}, u32[]{:S(2)}, u32[]{:S(2)}) %collective-permute-start.1) | collective-permute-done | bytes 393248 | tf_op jit(solution)/shard_map/ppermute | solution.py:21
  68.8 0.0 collective-permute-done
  68.8 0.1 pad_maximum_fusion
  68.9 0.1 fusion.66
  69.1 1.1 copy.40
  70.1 0.3 copy.42
  70.4 3.2 fusion.13
  73.6 124.7 %all-to-all-done = bf16[32,256,384]{1,2,0:T(8,128)(2,1)} async-done(((bf16[32,256,384]{1,2,0:T(8,128)(2,1)}), bf16[32,256,384]{1,2,0:T(8,128)(2,1)}, u32[]{:S(2)}, u32[]{:S(2)}) %all-to-all-start) | async-done | bytes 6291488 | tf_op jit(solution)/shard_map/all_to_all | solution.py:110
  198.3 9.0 %copy.46 = bf16[32,256,384]{1,0,2:T(8,128)(2,1)} copy(bf16[32,256,384]{1,2,0:T(8,128)(2,1)} %all-to-all-done) | data formatting | bytes 12582912 | tf_op jit(solution)/shard_map/all_to_all | solution.py:110
  207.3 10.5 %reshape_reshape.3 = bf16[8192,3,128]{0,2,1:T(8,128)(2,1)} reshape(bf16[32,256,384]{1,0,2:T(8,128)(2,1)} %copy.46) | data formatting | bytes 12582912 | tf_op jit(solution)/shard_map/reshape;reshape | solution.py:72
  217.8 15.0 %fusion = (f32[3,256]{1,0:T(4,128)S(1)}, f32[3,256,8192]{2,1,0:T(8,128)}) fusion(pred[256,8192]{1,0:T(8,128)(4,1)} %fusion.8, bf16[8192,3,128]{0,2,1:T(8,128)(2,1)} %bitcast.81, f32[256,3,128]{0,2,1:T(8,128)S(1)} %copy-done.5, f32[3,128]{1,0:T(4,128)S(1)} %bitcast.79, f32[256,3]{0,1:T(4,128)S(1)} %add_rsqrt_fusion), kind=kOutput, calls=%fused_computation.1 | convolution fusion | flops 1623588096 | bytes 33955328 | tf_op jit(solution)/shard_map/qhd,khd->hqk/dot_general | solution.py:73
  232.8 12.9 %fusion.2 = f32[3,128,256]{2,1,0:T(8,128)S(1)} fusion(bf16[8192,3,128]{0,2,1:T(8,128)(2,1)} %reshape_reshape.3, f32[3,256,8192]{2,1,0:T(8,128)} %get-tuple-element.15, pred[256,8192]{1,0:T(8,128)(4,1)} %fusion.8), kind=kOutput, calls=%fused_computation.3 | convolution fusion | flops 1623195648 | bytes 33947648 | tf_op jit(solution)/shard_map/hqk,khd->qhd/dot_general | solution.py:75
  245.7 2.3 fusion.24
  247.9 2.2 fusion.9
  250.1 2.6 copy.53
  252.7 0.0 reduce-scatter.4.cloned.1.call-update
  252.7 52.8 %reduce-scatter.4.cloned.1.call-done = bf16[384,256]{1,0:T(8,128)(2,1)} async-done(((bf16[3072,256]{1,0:T(8,128)(2,1)}), bf16[384,256]{1,0:T(8,128)(2,1)}) %reduce-scatter.4.cloned.1.call-update) | async-done | bytes 196624
  305.5 1.1 copy.54
  306.6 0.0 copy-start.3
  306.6 0.1 convert_reduce_fusion
  306.7 17.4 %psum.7 = f32[256]{0:T(256)} all-reduce(f32[256]{0:T(256)S(1)} %broadcast_multiply_fusion), channel_id=1, replica_groups=mesh['frame'=32,'head'=8] {'head'}, use_global_device_ids=true, to_apply=%region_8.9 | all-reduce | flops 256 | bytes 2048 | tf_op jit(solution)/shard_map/psum | solution.py:128
  (30 shorter events, 0.2 us)
Async XLA Ops:
  7.2 240.8 %copy-start = (bf16[384,3072]{1,0:T(8,128)(2,1)S(1)}, bf16[384,3072]{1,0:T(8,128)(2,1)}, u32[]{:S(2)}) copy-start(bf16[384,3072]{1,0:T(8,128)(2,1)} %param.10) | copy-start | bytes 7077892
  14.0 184.3 %all-to-all-start = ((bf16[32,256,384]{1,2,0:T(8,128)(2,1)}), bf16[32,256,384]{1,2,0:T(8,128)(2,1)}, u32[]{:S(2)}, u32[]{:S(2)}) async-start(bf16[32,256,384]{1,2,0:T(8,128)(2,1)} %stack.8), calls=%async_computation | async-start | bytes 12582912 | tf_op jit(solution)/shard_map/all_to_all | solution.py:110
  25.7 192.1 %all-gather.2.cloned.1.call-start = ((), (), s32[]{:S(2)}) async-start(), calls=%async_computation.2 | async-start | bytes 6488064 | tf_op jit(solution)/shard_map/all_gather | solution.py:108
  35.0 3.0 copy-start.6
  38.9 266.6 %reduce-scatter.4.cloned.1.call-start = ((), (), s32[]{:S(2)}) async-start(), calls=%async_computation.3 | async-start | bytes 1769472
  40.8 28.0 %collective-permute-start.1 = (bf16[2,256,384]{2,1,0:T(8,128)(2,1)}, bf16[2,256,384]{2,1,0:T(8,128)(2,1)S(1)}, u32[]{:S(2)}, u32[]{:S(2)}) collective-permute-start(bf16[2,256,384]{2,1,0:T(8,128)(2,1)} %pad_maximum_fusion.1), channel_id=1, source_target_pairs={{8,0},{16,8},{24,16},{32,24},{40,32},{48,40},{56,48},{64,56},{72,6... | collective-permute-start | bytes 1179656 | tf_op jit(solution)/shard_map/ppermute | solution.py:21
  42.9 26.0 %collective-permute-start = (bf16[2,256,384]{2,1,0:T(8,128)(2,1)}, bf16[2,256,384]{2,1,0:T(8,128)(2,1)S(1)}, u32[]{:S(2)}, u32[]{:S(2)}) collective-permute-start(bf16[2,256,384]{2,1,0:T(8,128)(2,1)} %pad_maximum_fusion.1), channel_id=1, source_target_pairs={{0,8},{8,16},{16,24},{24,32},{32,40},{40,48},{48,56},{56,64},{64,7... | collective-permute-start | bytes 1179656 | tf_op jit(solution)/shard_map/ppermute | solution.py:19
  45.4 4.4 %copy-start.7 = (s32[32]{0:T(128)S(1)}, s32[32]{0:T(128)}, u32[]{:S(2)}) copy-start(s32[32]{0:T(128)} %param.13) | copy-start | bytes 388
  45.4 4.7 %copy-start.8 = (s32[2,64]{1,0:T(2,128)S(1)}, s32[2,64]{1,0:T(2,128)}, u32[]{:S(2)}) copy-start(s32[2,64]{1,0:T(2,128)} %param.12) | copy-start | bytes 1540
  49.7 4.8 %copy-start.9 = (s32[2,4]{1,0:T(2,128)S(1)}, s32[2,4]{1,0:T(2,128)}, u32[]{:S(2)}) copy-start(s32[2,4]{1,0:T(2,128)} %param.11) | copy-start | bytes 100
  49.7 5.8 %copy-start.1 = (bf16[384,3072]{1,0:T(8,128)(2,1)S(1)}, bf16[384,3072]{1,0:T(8,128)(2,1)}, u32[]{:S(2)}) copy-start(bf16[384,3072]{1,0:T(8,128)(2,1)} %copy.41) | copy-start | bytes 7077892
  207.3 10.5 %copy-start.5 = (f32[256,3,128]{0,2,1:T(8,128)S(1)}, f32[256,3,128]{0,2,1:T(8,128)}, u32[]{:S(2)}) copy-start(f32[256,3,128]{0,2,1:T(8,128)} %get-tuple-element.11) | copy-start | bytes 1179652
  232.8 12.9 %copy-start.2 = (pred[256,768]{1,0:T(8,128)(4,1)S(1)}, pred[256,768]{1,0:T(8,128)(4,1)}, u32[]{:S(2)}) copy-start(pred[256,768]{1,0:T(8,128)(4,1)} %fusion.34) | copy-start | bytes 589828
  232.8 12.9 %copy-start.4 = (bf16[1,768,384]{1,2,0:T(8,128)(2,1)S(1)}, bf16[1,768,384]{1,2,0:T(8,128)(2,1)}, u32[]{:S(2)}) copy-start(bf16[1,768,384]{1,2,0:T(8,128)(2,1)} %copy.40) | copy-start | bytes 1769476
  306.6 17.6 %copy-start.3 = (bf16[384,256]{0,1:T(8,128)(2,1)}, bf16[384,256]{0,1:T(8,128)(2,1)S(1)}, u32[]{:S(2)}) copy-start(bf16[384,256]{0,1:T(8,128)(2,1)S(1)} %copy.54) | copy-start | bytes 589828
Sparse Core Ops, SparseCore 0:
  39.0 151.3 all-gather.1
  252.8 52.6 reduce-scatter.3
